TPU v7x, 32 devices: a whole 2x2x4 slice. The times are simulated.
32 devices in a mesh: cuts: 2 (over x), tile: 16 (over z, y, core).
Axes of the slice: x: 2, y: 2, z: 4, core: 2. Of those that a mesh axis runs over, the one named last changes fastest.
Arguments:
- object_delta: float32 [2, 2, 2048, 4096], P('cuts', None, None, 'tile'), may hold values from -1.2 to 1.2
- probe_wave: bfloat16 [2, 256, 256], replicated, may hold values from -4 to 4
- intensity: float32 [32, 256, 256], P('tile'), may hold values from 0 to 2
- positions: int32 [32, 2], P('tile'), may hold values from 0 to 3840, as said below
Outputs:
- object_gradient: float32 [2, 2, 2048, 4096], P('cuts', None, None, 'tile')
Inputs may be any that keep to these rules, and one draw needn't show every extreme that they name: `positions`: row entries run from 0 to 1792. The column of probe k lies in columns (k // 2) * 256 to (k // 2) * 256 + 255, and equals (k // 2) * 256 for the probes of the last block of 2.
All inputs are finite; a program needn't handle non-finite values.
Results may differ from a plain program's by a relative error of at most 0.04.
Values may be sent and summed in bfloat16 or wider, within the bound.
A program may use at most 64 MiB of HBM per device.

v0:
```python
import functools
import math

import jax
import jax.numpy as jnp
import numpy as np
from jax import lax
from jax.experimental import pallas as pl
from jax.experimental.pallas import tpu as pltpu
from jax.sharding import PartitionSpec as P

F32 = jnp.float32
BF16 = jnp.bfloat16
MESH = pl.DeviceIdType.MESH
LANE_ROWS = 8


def make_tables(width):
    counter = np.arange(width)
    phase = (counter[:, None] * counter[None, :] % width) * (2.0 * math.pi / width)
    four = np.exp(-1j * phase) / math.sqrt(width)
    signed = np.where(counter < width // 2, counter, counter - width).astype(np.float64)
    kernel = np.exp(-2j * math.pi / width * signed * signed)
    prop = np.conj(four) @ (kernel[:, None] * four)
    prop = 0.5 * (prop + prop.T)

    def block(table):
        re, im = table.real, table.imag
        return np.block([[re, -im], [im, re]])

    big = [block(prop), block(prop).T, block(four), block(four).T]
    return np.stack(big).astype(np.float32).astype(jnp.bfloat16)


def dot(a, b):
    return jnp.dot(a, b, preferred_element_type=F32)


def repeat(count, body):
    if count == 1:
        body(0)
    elif count > 1:
        lax.fori_loop(0, count, lambda i, _: (body(i), 0)[1], 0)


def exchange_kernel(
    obj_hbm, probe_hbm, inten_hbm, pos, tabs_hbm,
    own_out, strip_out, left_out,
    obj_v, obj_b, probe_v, inten_v, tabs_v, strip_send, strip_recv, win, psi, lam, grad_send,
    load_sem, pos_sem, strip_ssem, strip_rsem, x_ssem, x_rsem, g_ssem, g_rsem,
    *, chunks, gchunks,
):
    cut, tile = lax.axis_index("cuts"), lax.axis_index("tile")
    ncut, ntile = lax.axis_size("cuts"), lax.axis_size("tile")
    per, _, rows, cols = obj_v.shape
    count, width = inten_v.shape[0], inten_v.shape[1]
    total = ncut * per
    height = width // chunks
    gheight = width // gchunks
    has_left, has_right = tile > 0, tile < ntile - 1
    left, right = {"tile": tile - 1}, {"tile": tile + 1}

    obj_copy = pltpu.make_async_copy(obj_hbm, obj_v, load_sem.at[0])
    probe_copy = pltpu.make_async_copy(probe_hbm, probe_v, load_sem.at[1])
    tabs_copy = pltpu.make_async_copy(tabs_hbm, tabs_v, load_sem.at[2])
    inten_copy = pltpu.make_async_copy(inten_hbm, inten_v, load_sem.at[3])
    obj_copy.start()
    probe_copy.start()
    tabs_copy.start()
    inten_copy.start()

    barrier = pltpu.get_barrier_semaphore()

    @pl.when(has_left)
    def _():
        pl.semaphore_signal(barrier, inc=1, device_id=left, device_id_type=MESH)

    @pl.when(has_right)
    def _():
        pl.semaphore_signal(barrier, inc=1, device_id=right, device_id_type=MESH)

    for o in range(1, ncut):
        peer = {"cuts": lax.rem(cut + o, ncut)}
        pl.semaphore_signal(barrier, inc=1, device_id=peer, device_id_type=MESH)
    peers = ncut - 1 + jnp.where(has_left, 1, 0) + jnp.where(has_right, 1, 0)
    pl.semaphore_wait(barrier, peers)

    pos_copy = pltpu.make_async_remote_copy(
        src_ref=pos, dst_ref=left_out, send_sem=pos_sem.at[0], recv_sem=pos_sem.at[1],
        device_id=right, device_id_type=MESH,
    )

    @pl.when(has_right)
    def _():
        pos_copy.start()

    lanes = lax.broadcasted_iota(jnp.int32, (height, cols), 1)
    glanes = lax.broadcasted_iota(jnp.int32, (gheight, cols), 1)
    cell = lax.broadcasted_iota(jnp.int32, (width, rows), 1)
    line = lax.broadcasted_iota(jnp.int32, (width, rows), 0)

    def window_rows(row):
        base = row // LANE_ROWS * LANE_ROWS
        wanted = base + line + jnp.where(line < row - base, width, 0)
        pick = jnp.where(cell == wanted, 1.0, 0.0).astype(BF16)
        return dot(pick, obj_b[...]).astype(BF16)

    def strip_copy(p, k):
        span = pl.ds(k * height, height)
        return pltpu.make_async_remote_copy(
            src_ref=strip_send.at[p, :, :, span, :], dst_ref=strip_recv.at[p, :, :, span, :],
            send_sem=strip_ssem.at[p, k], recv_sem=strip_rsem.at[p, k],
            device_id=left, device_id_type=MESH,
        )

    def cross_copy(o, source, p, k):
        span = pl.ds(k * height, height)
        part = win.at[p, source, :, :, span, :]
        return pltpu.make_async_remote_copy(
            src_ref=part, dst_ref=part,
            send_sem=x_ssem.at[o - 1, p, k], recv_sem=x_rsem.at[o - 1, p, k],
            device_id={"cuts": lax.rem(cut + o, ncut)}, device_id_type=MESH,
        )

    def grad_copy(p, k):
        span = pl.ds(k * gheight, gheight)
        return pltpu.make_async_remote_copy(
            src_ref=grad_send.at[p, :, :, span, :], dst_ref=strip_out.at[p, :, :, span, :],
            send_sem=g_ssem.at[p, k], recv_sem=g_rsem.at[p, k],
            device_id=right, device_id_type=MESH,
        )

    probe_copy.wait()
    across = lax.broadcasted_iota(jnp.int32, (width, width), 1)
    down = lax.broadcasted_iota(jnp.int32, (width, width), 0)
    for p in range(count):
        row, col = pos[p, 0], pos[p, 1] - tile * cols
        shift = row - row // LANE_ROWS * LANE_ROWS
        source = across + shift
        move_rows = jnp.where(jnp.where(source >= width, source - width, source) == down, 1.0, 0.0)
        source = down + col
        move_cols = jnp.where(jnp.where(source >= width, source - width, source) == across, 1.0, 0.0)
        for part in range(2):
            moved = dot(move_rows.astype(BF16), probe_v[part]).astype(BF16)
            psi[p, 0, part] = dot(moved, move_cols.astype(BF16)).astype(BF16)

    obj_copy.wait()
    for j in range(per):
        for part in range(2):
            side = pl.ds((2 * j + part) * cols, cols)
            obj_b[:, side] = obj_v[j, part].astype(BF16)

    @pl.when(has_left)
    def _():
        pos_copy.wait_recv()
        for p in range(count):
            picked = window_rows(left_out[p, 0])
            for j in range(per):
                for part in range(2):
                    first = (2 * j + part) * cols
                    strip_send[p, j, part] = picked[:, first : first + cols]
            for k in range(chunks):
                strip_copy(p, k).start()

    @pl.when(jnp.logical_not(has_left))
    def _():
        for p in range(count):
            for d in range(2):
                left_out[p, d] = 0
        strip_out[...] = jnp.zeros_like(strip_out)

    @pl.when(jnp.logical_not(has_right))
    def _():
        strip_recv[...] = jnp.zeros_like(strip_recv)

    for p in range(count):
        picked = window_rows(pos[p, 0])
        for j in range(per):
            for part in range(2):
                first = (2 * j + part) * cols
                win[p, cut, j, part] = picked[:, first : first + cols]

    for p in range(count):
        col = pos[p, 1] - tile * cols
        for k in range(chunks):

            @pl.when(has_right)
            def _():
                strip_copy(p, k).wait_recv()

            span = pl.ds(k * height, height)
            for j in range(per):
                for part in range(2):
                    win[p, cut, j, part, span, :] = jnp.where(
                        lanes >= col,
                        win[p, cut, j, part, span, :].astype(F32),
                        strip_recv[p, j, part, span, :].astype(F32),
                    ).astype(BF16)
            for o in range(1, ncut):
                cross_copy(o, cut, p, k).start()

    tabs_copy.wait()
    inten_copy.wait()

    def arrive(p, owner):
        @pl.when(owner != cut)
        def _():
            o = lax.rem(cut - owner + ncut, ncut)
            for k in range(chunks):
                cross_copy(o, owner, p, k).wait_recv()

    def sandwich(first, second, stacked):
        inner = dot(tabs_v[first], stacked).astype(BF16)
        side = jnp.concatenate([inner[:width], inner[width:]], axis=1)
        return dot(side, tabs_v[second])

    def exit_wave(p, s):
        owner, j = s // per, lax.rem(s, per)
        t_re = 1.0 + win[p, owner, j, 0].astype(F32)
        t_im = win[p, owner, j, 1].astype(F32)
        p_re, p_im = psi[p, s, 0].astype(F32), psi[p, s, 1].astype(F32)
        x_re = (p_re * t_re - p_im * t_im).astype(BF16)
        x_im = (p_re * t_im + p_im * t_re).astype(BF16)
        return jnp.concatenate([x_re, x_im], axis=0)

    def adjoint_slice(p, s, first, second, stacked):
        owner, j = s // per, lax.rem(s, per)
        col = pos[p, 1] - tile * cols
        inner = dot(tabs_v[first], stacked).astype(BF16)
        side = jnp.concatenate([inner[:width], inner[width:]], axis=1)

        @pl.when(owner == cut)
        def _():
            for k in range(gchunks):
                span = pl.ds(k * gheight, gheight)
                mu = dot(side[k * gheight : (k + 1) * gheight], tabs_v[second])
                m_re, m_im = mu[:, :width], mu[:, width:]
                p_re = psi[p, s, 0, span, :].astype(F32)
                p_im = psi[p, s, 1, span, :].astype(F32)
                g = (p_re * m_re + p_im * m_im, p_re * m_im - p_im * m_re)
                for part in range(2):
                    own_out[p, j, part, span, :] = jnp.where(glanes >= col, g[part], 0.0)
                    grad_send[p, j, part, span, :] = jnp.where(glanes >= col, 0.0, g[part]).astype(
                        BF16
                    )
                if per == 1:

                    @pl.when(has_right)
                    def _():
                        grad_copy(p, k).start()

        @pl.when(s > cut * per)
        def _():
            mu = dot(side, tabs_v[second])
            m_re, m_im = mu[:, :width], mu[:, width:]
            t_re = 1.0 + win[p, owner, j, 0].astype(F32)
            t_im = win[p, owner, j, 1].astype(F32)
            lam[:width] = (t_re * m_re + t_im * m_im).astype(BF16)
            lam[width:] = (t_re * m_im - t_im * m_re).astype(BF16)

    def one_probe(p):
        def forward(s):
            arrive(p, s // per)
            out = sandwich(0, 1, exit_wave(p, s))
            psi[p, s + 1, 0] = out[:, :width].astype(BF16)
            psi[p, s + 1, 1] = out[:, width:].astype(BF16)

        def backward(i):
            s = total - 2 - i

            @pl.when(s >= cut * per)
            def _():
                adjoint_slice(p, s, 1, 0, lam[...])

        if per == 1:
            repeat(total - 1, forward)
            arrive(p, total - 1)
        else:
            for s in range(ncut):
                arrive(p, s)
        adjoint_slice(p, total - 1, 3, 2, far_field(p))
        repeat(total - 1, backward)
        if per > 1:
            for k in range(gchunks):

                @pl.when(has_right)
                def _():
                    grad_copy(p, k).start()

    def far_field(p):
        out = sandwich(2, 3, exit_wave(p, total - 1))
        f_re, f_im = out[:, :width], out[:, width:]
        misfit = f_re * f_re + f_im * f_im - inten_v[p]
        return jnp.concatenate([(misfit * f_re).astype(BF16), (misfit * f_im).astype(BF16)], axis=0)

    for p in range(count):
        one_probe(p)

    @pl.when(has_right)
    def _():
        pos_copy.wait_send()
        for p in range(count):
            for k in range(gchunks):
                grad_copy(p, k).wait_send()

    for p in range(count):
        for k in range(chunks):
            for o in range(1, ncut):
                cross_copy(o, cut, p, k).wait_send()

    @pl.when(has_left)
    def _():
        for p in range(count):
            for k in range(chunks):
                strip_copy(p, k).wait_send()
        for p in range(count):
            for k in range(gchunks):
                grad_copy(p, k).wait_recv()


def place_kernel(own, strip, pos, left, out_hbm, out_v, sem):
    per, _, rows, cols = out_v.shape
    count, width = own.shape[0], own.shape[3]
    out_v[...] = jnp.zeros_like(out_v)
    iota = lax.broadcasted_iota(jnp.int32, (LANE_ROWS, cols), 0)

    def add(source, row, p):
        base = row // LANE_ROWS * LANE_ROWS
        shift = row - base
        body = pl.multiple_of(base + LANE_ROWS, LANE_ROWS)
        base = pl.multiple_of(base, LANE_ROWS)
        after = pl.multiple_of(jnp.minimum(base + width, rows - LANE_ROWS), LANE_ROWS)
        rest = width - LANE_ROWS
        for j in range(per):
            for part in range(2):
                whole = source[p, j, part].astype(F32)
                out_v[j, part, pl.ds(body, rest), :] += whole[LANE_ROWS:]
                head = whole[:LANE_ROWS]
                out_v[j, part, pl.ds(base, LANE_ROWS), :] += jnp.where(iota >= shift, head, 0.0)
                out_v[j, part, pl.ds(after, LANE_ROWS), :] += jnp.where(iota < shift, head, 0.0)

    for p in range(count):
        add(own, pos[p, 0], p)
        add(strip, left[p, 0], p)
    copy = pltpu.make_async_copy(out_v, out_hbm, sem)
    copy.start()
    copy.wait()


def per_device(tables, object_delta, probe_wave, intensity, positions):
    per, _, rows, cols = object_delta.shape
    count, width = intensity.shape[0], intensity.shape[1]
    ncut = lax.axis_size("cuts")
    chunks, gchunks = 4, 2
    anywhere = pl.BlockSpec(memory_space=pl.ANY)
    vmem = pl.BlockSpec(memory_space=pltpu.VMEM)
    smem = pl.BlockSpec(memory_space=pltpu.SMEM)
    dma = pltpu.SemaphoreType.DMA
    piece = (count, per, 2, width, cols)
    others = max(ncut - 1, 1)
    own, strip, left = pl.pallas_call(
        functools.partial(exchange_kernel, chunks=chunks, gchunks=gchunks),
        out_shape=(
            jax.ShapeDtypeStruct(piece, F32),
            jax.ShapeDtypeStruct(piece, BF16),
            jax.ShapeDtypeStruct(positions.shape, positions.dtype),
        ),
        in_specs=[anywhere, anywhere, anywhere, smem, anywhere],
        out_specs=(vmem, vmem, smem),
        scratch_shapes=[
            pltpu.VMEM(object_delta.shape, F32),
            pltpu.VMEM((rows, per * 2 * cols), BF16),
            pltpu.VMEM(probe_wave.shape, BF16),
            pltpu.VMEM(intensity.shape, F32),
            pltpu.VMEM(tables.shape, BF16),
            pltpu.VMEM(piece, BF16),
            pltpu.VMEM(piece, BF16),
            pltpu.VMEM((count, ncut, per, 2, width, cols), BF16),
            pltpu.VMEM((count, ncut * per, 2, width, cols), BF16),
            pltpu.VMEM((2 * width, cols), BF16),
            pltpu.VMEM(piece, BF16),
            dma((4,)),
            dma((2,)),
            dma((count, chunks)),
            dma((count, chunks)),
            dma((others, count, chunks)),
            dma((others, count, chunks)),
            dma((count, gchunks)),
            dma((count, gchunks)),
        ],
        compiler_params=pltpu.CompilerParams(collective_id=0, has_side_effects=True),
        name="exchange",
    )(object_delta, probe_wave, intensity, positions, tables)
    return pl.pallas_call(
        place_kernel,
        out_shape=jax.ShapeDtypeStruct(object_delta.shape, F32),
        in_specs=[vmem, vmem, smem, smem],
        out_specs=anywhere,
        scratch_shapes=[pltpu.VMEM(object_delta.shape, F32), dma],
        name="place",
    )(own, strip, positions, left)


def solution(mesh):
    def whole(object_delta, probe_wave, intensity, positions):
        tables = jnp.asarray(make_tables(probe_wave.shape[-1]))
        return jax.shard_map(
            per_device,
            mesh=mesh,
            in_specs=(
                P(),
                P("cuts", None, None, "tile"),
                P(),
                P("tile", None, None),
                P("tile", None),
            ),
            out_specs=P("cuts", None, None, "tile"),
            check_vma=False,
        )(tables, object_delta, probe_wave, intensity, positions)

    return whole
```

profile of v0, /device:TPU:24, one launch (start us, length us, event | category | flops | bytes accessed | tf_op | source)
XLA Modules:
  0.0 33.3 jit_solution(5138940149647311350)
XLA Ops:
  0.0 29.4 %exchange.1 = (f32[2,1,2,256,256]{4,3,2,1,0:T(8,128)}, bf16[2,1,2,256,256]{4,3,2,1,0:T(8,128)(2,1)}, s32[2,2]{1,0:T(2,128)}) custom-call(f32[1,2,2048,256]{3,2,1,0:T(8,128)} %obj_hbm.1, bf16[2,256,256]{2,1,0:T(8,128)(2,1)} %probe_hbm.1, f32[2,256,256]{2,1,0:T(8,128)} %inten_hbm.1, s32[2,2]{1,0:T(2,128)} %pos.3, bf16[4,512,512]{2,1,0:T(8,128)(2,1)} %constant.2.clone.tabs_hbm), custom_call_target="tpu_custom_call" | custom-call | tf_op jit(solution)/shard_map/exchange/pallas_call | solution.py:361
  29.4 3.9 %place.1 = f32[1,2,2048,256]{3,2,1,0:T(8,128)} custom-call(f32[2,1,2,256,256]{4,3,2,1,0:T(8,128)} %get-tuple-element.8.own, bf16[2,1,2,256,256]{4,3,2,1,0:T(8,128)(2,1)} %get-tuple-element.9.strip, s32[2,2]{1,0:T(2,128)} %pos.3, s32[2,2]{1,0:T(2,128)} %get-tuple-element.10.left), custom_call_target="tpu_custom_call" | custom-call | tf_op jit(solution)/shard_map/place/pallas_call | solution.py:394
where the time goes:
time: 33.5 us; the launch traced here: 33.3 us
  Pallas kernels  33.3 us (99%)
    pallas_call x1, Pallas kernels, per_device(): pl.pallas_call(functools.partial(exchange_kernel, chunks=chunks, gchunks=...  29.4 us
    pallas_call x1, Pallas kernels, per_device(): pl.pallas_call(place_kernel, out_shape=jax.ShapeDtypeStruct(object_delta....  3.9 us

commit v1 on v0

--- a/solution.py
+++ b/solution.py
@@ -47,7 +47,7 @@
     obj_hbm, probe_hbm, inten_hbm, pos, tabs_hbm,
     own_out, strip_out, left_out,
     obj_v, obj_b, probe_v, inten_v, tabs_v, strip_send, strip_recv, win, psi, lam, grad_send,
-    load_sem, pos_sem, strip_ssem, strip_rsem, x_ssem, x_rsem, g_ssem, g_rsem,
+    obj_sem, load_sem, pos_sem, strip_ssem, strip_rsem, x_ssem, x_rsem, g_ssem, g_rsem,
     *, chunks, gchunks,
 ):
     cut, tile = lax.axis_index("cuts"), lax.axis_index("tile")
@@ -60,14 +60,16 @@
     has_left, has_right = tile > 0, tile < ntile - 1
     left, right = {"tile": tile - 1}, {"tile": tile + 1}
 
-    obj_copy = pltpu.make_async_copy(obj_hbm, obj_v, load_sem.at[0])
+    def obj_copy(j, part):
+        return pltpu.make_async_copy(obj_hbm.at[j, part], obj_v.at[j, part], obj_sem.at[j, part])
+
     probe_copy = pltpu.make_async_copy(probe_hbm, probe_v, load_sem.at[1])
     tabs_copy = pltpu.make_async_copy(tabs_hbm, tabs_v, load_sem.at[2])
     inten_copy = pltpu.make_async_copy(inten_hbm, inten_v, load_sem.at[3])
-    obj_copy.start()
+    for j in range(per):
+        for part in range(2):
+            obj_copy(j, part).start()
     probe_copy.start()
-    tabs_copy.start()
-    inten_copy.start()
 
     barrier = pltpu.get_barrier_semaphore()
 
@@ -96,14 +98,15 @@
 
     lanes = lax.broadcasted_iota(jnp.int32, (height, cols), 1)
     glanes = lax.broadcasted_iota(jnp.int32, (gheight, cols), 1)
-    cell = lax.broadcasted_iota(jnp.int32, (width, rows), 1)
-    line = lax.broadcasted_iota(jnp.int32, (width, rows), 0)
+    unit = 128
+    cell = lax.broadcasted_iota(jnp.int32, (width, unit), 1)
+    line = lax.broadcasted_iota(jnp.int32, (width, unit), 0)
 
     def window_rows(row):
         base = row // LANE_ROWS * LANE_ROWS
-        wanted = base + line + jnp.where(line < row - base, width, 0)
-        pick = jnp.where(cell == wanted, 1.0, 0.0).astype(BF16)
-        return dot(pick, obj_b[...]).astype(BF16)
+        wanted = base + line + jnp.where(line < row - base, width, 0) - cell
+        picks = [jnp.where(wanted == i * unit, 1.0, 0.0).astype(BF16) for i in range(rows // unit)]
+        return dot(jnp.concatenate(picks, axis=1), obj_b[...]).astype(BF16)
 
     def strip_copy(p, k):
         span = pl.ds(k * height, height)
@@ -129,6 +132,64 @@
             send_sem=g_ssem.at[p, k], recv_sem=g_rsem.at[p, k],
             device_id=right, device_id_type=MESH,
         )
+
+    for j in range(per):
+        for part in range(2):
+            obj_copy(j, part).wait()
+            side = pl.ds((2 * j + part) * cols, cols)
+            obj_b[:, side] = obj_v[j, part].astype(BF16)
+
+    tabs_copy.start()
+    inten_copy.start()
+
+    @pl.when(has_left)
+    def _():
+        pos_copy.wait_recv()
+        for p in range(count):
+            picked = window_rows(left_out[p, 0])
+            for j in range(per):
+                for part in range(2):
+                    first = (2 * j + part) * cols
+                    strip_send[p, j, part] = picked[:, first : first + cols]
+            for k in range(chunks):
+                strip_copy(p, k).start()
+
+    @pl.when(jnp.logical_not(has_left))
+    def _():
+        for p in range(count):
+            for d in range(2):
+                left_out[p, d] = 0
+        strip_out[...] = jnp.zeros_like(strip_out)
+
+    @pl.when(jnp.logical_not(has_right))
+    def _():
+        strip_recv[...] = jnp.zeros_like(strip_recv)
+
+    for p in range(count):
+        picked = window_rows(pos[p, 0])
+        for j in range(per):
+            for part in range(2):
+                first = (2 * j + part) * cols
+                win[p, cut, j, part] = picked[:, first : first + cols]
+
+    for p in range(count):
+        col = pos[p, 1] - tile * cols
+        for k in range(chunks):
+
+            @pl.when(has_right)
+            def _():
+                strip_copy(p, k).wait_recv()
+
+            span = pl.ds(k * height, height)
+            for j in range(per):
+                for part in range(2):
+                    win[p, cut, j, part, span, :] = jnp.where(
+                        lanes >= col,
+                        win[p, cut, j, part, span, :].astype(F32),
+                        strip_recv[p, j, part, span, :].astype(F32),
+                    ).astype(BF16)
+            for o in range(1, ncut):
+                cross_copy(o, cut, p, k).start()
 
     probe_copy.wait()
     across = lax.broadcasted_iota(jnp.int32, (width, width), 1)
@@ -143,61 +204,6 @@
         for part in range(2):
             moved = dot(move_rows.astype(BF16), probe_v[part]).astype(BF16)
             psi[p, 0, part] = dot(moved, move_cols.astype(BF16)).astype(BF16)
-
-    obj_copy.wait()
-    for j in range(per):
-        for part in range(2):
-            side = pl.ds((2 * j + part) * cols, cols)
-            obj_b[:, side] = obj_v[j, part].astype(BF16)
-
-    @pl.when(has_left)
-    def _():
-        pos_copy.wait_recv()
-        for p in range(count):
-            picked = window_rows(left_out[p, 0])
-            for j in range(per):
-                for part in range(2):
-                    first = (2 * j + part) * cols
-                    strip_send[p, j, part] = picked[:, first : first + cols]
-            for k in range(chunks):
-                strip_copy(p, k).start()
-
-    @pl.when(jnp.logical_not(has_left))
-    def _():
-        for p in range(count):
-            for d in range(2):
-                left_out[p, d] = 0
-        strip_out[...] = jnp.zeros_like(strip_out)
-
-    @pl.when(jnp.logical_not(has_right))
-    def _():
-        strip_recv[...] = jnp.zeros_like(strip_recv)
-
-    for p in range(count):
-        picked = window_rows(pos[p, 0])
-        for j in range(per):
-            for part in range(2):
-                first = (2 * j + part) * cols
-                win[p, cut, j, part] = picked[:, first : first + cols]
-
-    for p in range(count):
-        col = pos[p, 1] - tile * cols
-        for k in range(chunks):
-
-            @pl.when(has_right)
-            def _():
-                strip_copy(p, k).wait_recv()
-
-            span = pl.ds(k * height, height)
-            for j in range(per):
-                for part in range(2):
-                    win[p, cut, j, part, span, :] = jnp.where(
-                        lanes >= col,
-                        win[p, cut, j, part, span, :].astype(F32),
-                        strip_recv[p, j, part, span, :].astype(F32),
-                    ).astype(BF16)
-            for o in range(1, ncut):
-                cross_copy(o, cut, p, k).start()
 
     tabs_copy.wait()
     inten_copy.wait()
@@ -321,30 +327,33 @@
 def place_kernel(own, strip, pos, left, out_hbm, out_v, sem):
     per, _, rows, cols = out_v.shape
     count, width = own.shape[0], own.shape[3]
-    out_v[...] = jnp.zeros_like(out_v)
     iota = lax.broadcasted_iota(jnp.int32, (LANE_ROWS, cols), 0)
-
-    def add(source, row, p):
+    rest = width - LANE_ROWS
+
+    def add(source, row, p, j, part):
         base = row // LANE_ROWS * LANE_ROWS
         shift = row - base
         body = pl.multiple_of(base + LANE_ROWS, LANE_ROWS)
         base = pl.multiple_of(base, LANE_ROWS)
         after = pl.multiple_of(jnp.minimum(base + width, rows - LANE_ROWS), LANE_ROWS)
-        rest = width - LANE_ROWS
-        for j in range(per):
-            for part in range(2):
-                whole = source[p, j, part].astype(F32)
-                out_v[j, part, pl.ds(body, rest), :] += whole[LANE_ROWS:]
-                head = whole[:LANE_ROWS]
-                out_v[j, part, pl.ds(base, LANE_ROWS), :] += jnp.where(iota >= shift, head, 0.0)
-                out_v[j, part, pl.ds(after, LANE_ROWS), :] += jnp.where(iota < shift, head, 0.0)
-
-    for p in range(count):
-        add(own, pos[p, 0], p)
-        add(strip, left[p, 0], p)
-    copy = pltpu.make_async_copy(out_v, out_hbm, sem)
-    copy.start()
-    copy.wait()
+        whole = source[p, j, part].astype(F32)
+        out_v[j, part, pl.ds(body, rest), :] += whole[LANE_ROWS:]
+        head = whole[:LANE_ROWS]
+        out_v[j, part, pl.ds(base, LANE_ROWS), :] += jnp.where(iota >= shift, head, 0.0)
+        out_v[j, part, pl.ds(after, LANE_ROWS), :] += jnp.where(iota < shift, head, 0.0)
+
+    copies = []
+    for j in range(per):
+        for part in range(2):
+            out_v[j, part] = jnp.zeros((rows, cols), F32)
+            for p in range(count):
+                add(own, pos[p, 0], p, j, part)
+                add(strip, left[p, 0], p, j, part)
+            copy = pltpu.make_async_copy(out_v.at[j, part], out_hbm.at[j, part], sem.at[j, part])
+            copy.start()
+            copies.append(copy)
+    for copy in copies:
+        copy.wait()
 
 
 def per_device(tables, object_delta, probe_wave, intensity, positions):
@@ -361,8 +370,8 @@
     own, strip, left = pl.pallas_call(
         functools.partial(exchange_kernel, chunks=chunks, gchunks=gchunks),
         out_shape=(
-            jax.ShapeDtypeStruct(piece, F32),
-            jax.ShapeDtypeStruct(piece, BF16),
+            pltpu.VMEM(piece, F32),
+            pltpu.VMEM(piece, BF16),
             jax.ShapeDtypeStruct(positions.shape, positions.dtype),
         ),
         in_specs=[anywhere, anywhere, anywhere, smem, anywhere],
@@ -379,6 +388,7 @@
             pltpu.VMEM((count, ncut * per, 2, width, cols), BF16),
             pltpu.VMEM((2 * width, cols), BF16),
             pltpu.VMEM(piece, BF16),
+            dma((per, 2)),
             dma((4,)),
             dma((2,)),
             dma((count, chunks)),
@@ -391,12 +401,14 @@
         compiler_params=pltpu.CompilerParams(collective_id=0, has_side_effects=True),
         name="exchange",
     )(object_delta, probe_wave, intensity, positions, tables)
+    own = pltpu.with_memory_space_constraint(own, pltpu.VMEM)
+    strip = pltpu.with_memory_space_constraint(strip, pltpu.VMEM)
     return pl.pallas_call(
         place_kernel,
         out_shape=jax.ShapeDtypeStruct(object_delta.shape, F32),
         in_specs=[vmem, vmem, smem, smem],
         out_specs=anywhere,
-        scratch_shapes=[pltpu.VMEM(object_delta.shape, F32), dma],
+        scratch_shapes=[pltpu.VMEM(object_delta.shape, F32), dma((per, 2))],
         name="place",
     )(own, strip, positions, left)
 

time: 33.5 us -> 32 us (0.955)
  Pallas kernels: 33.3 us -> 31.8 us
    pallas_call x1, Pallas kernels: 3.9 us -> 2.99 us  [per_device(): pl.pallas_call(place_kernel, out_shape=jax.ShapeDtypeStruct(object_delta....]
    pallas_call x1, Pallas kernels: 29.4 us -> 28.8 us  [per_device(): pl.pallas_call(functools.partial(exchange_kernel, chunks=chunks, gchunks=...]
where the time goes in v1:
time: 32 us; the launch traced here: 31.8 us
  Pallas kernels  31.8 us (99%)
    pallas_call x1, Pallas kernels, per_device(): pl.pallas_call(functools.partial(exchange_kernel, chunks=chunks, gchunks=...  28.8 us
    pallas_call x1, Pallas kernels, per_device(): pl.pallas_call(place_kernel, out_shape=jax.ShapeDtypeStruct(object_delta....  2.99 us

profile of v1, /device:TPU:24, one launch (start us, length us, event | category | flops | bytes accessed | tf_op | source)
XLA Modules:
  0.0 31.8 jit_solution(3803623524164567602)
XLA Ops:
  0.0 28.8 %exchange.1 = (f32[2,1,2,256,256]{4,3,2,1,0:T(8,128)S(1)}, bf16[2,1,2,256,256]{4,3,2,1,0:T(8,128)(2,1)S(1)}, s32[2,2]{1,0:T(2,128)}) custom-call(f32[1,2,2048,256]{3,2,1,0:T(8,128)} %obj_hbm.1, bf16[2,256,256]{2,1,0:T(8,128)(2,1)} %probe_hbm.1, f32[2,256,256]{2,1,0:T(8,128)} %inten_hbm.1, s32[2,2]{1,0:T(2,128)} %pos.3, ...), custom_call_target="tpu_custom_call" | custom-call | tf_op jit(solution)/shard_map/exchange/pallas_call | solution.py:370
  28.8 3.0 %place.1 = f32[1,2,2048,256]{3,2,1,0:T(8,128)} custom-call(f32[2,1,2,256,256]{4,3,2,1,0:T(8,128)S(1)} %get-tuple-element.8.own, bf16[2,1,2,256,256]{4,3,2,1,0:T(8,128)(2,1)S(1)} %get-tuple-element.9.strip, s32[2,2]{1,0:T(2,128)} %pos.3, s32[2,2]{1,0:T(2,128)} %get-tuple-element.10.left), custom_call_target="tpu_custom_call" | custom-call | tf_op jit(solution)/shard_map/place/pallas_call | solution.py:406

commit v2 on v1

--- a/solution.py
+++ b/solution.py
@@ -102,9 +102,10 @@
     cell = lax.broadcasted_iota(jnp.int32, (width, unit), 1)
     line = lax.broadcasted_iota(jnp.int32, (width, unit), 0)
 
-    def window_rows(row):
+    def window_rows(row, first=0, size=width):
         base = row // LANE_ROWS * LANE_ROWS
         wanted = base + line + jnp.where(line < row - base, width, 0) - cell
+        wanted = wanted[first : first + size]
         picks = [jnp.where(wanted == i * unit, 1.0, 0.0).astype(BF16) for i in range(rows // unit)]
         return dot(jnp.concatenate(picks, axis=1), obj_b[...]).astype(BF16)
 
@@ -146,13 +147,18 @@
     def _():
         pos_copy.wait_recv()
         for p in range(count):
-            picked = window_rows(left_out[p, 0])
-            for j in range(per):
-                for part in range(2):
-                    first = (2 * j + part) * cols
-                    strip_send[p, j, part] = picked[:, first : first + cols]
-            for k in range(chunks):
-                strip_copy(p, k).start()
+            steps = 2 if p == 0 else 1
+            size = width // steps
+            for step in range(steps):
+                picked = window_rows(left_out[p, 0], step * size, size)
+                for j in range(per):
+                    for part in range(2):
+                        first = (2 * j + part) * cols
+                        strip_send[p, j, part, pl.ds(step * size, size), :] = picked[
+                            :, first : first + cols
+                        ]
+                for k in range(step * chunks // steps, (step + 1) * chunks // steps):
+                    strip_copy(p, k).start()
 
     @pl.when(jnp.logical_not(has_left))
     def _():
@@ -171,8 +177,6 @@
             for part in range(2):
                 first = (2 * j + part) * cols
                 win[p, cut, j, part] = picked[:, first : first + cols]
-
-    for p in range(count):
         col = pos[p, 1] - tile * cols
         for k in range(chunks):
 
@@ -360,7 +364,7 @@
     per, _, rows, cols = object_delta.shape
     count, width = intensity.shape[0], intensity.shape[1]
     ncut = lax.axis_size("cuts")
-    chunks, gchunks = 4, 2
+    chunks, gchunks = 8, 4
     anywhere = pl.BlockSpec(memory_space=pl.ANY)
     vmem = pl.BlockSpec(memory_space=pltpu.VMEM)
     smem = pl.BlockSpec(memory_space=pltpu.SMEM)

time: 32 us -> 32 us (level)
  no operation moved by 1% of the time
where the time goes in v2:
time: 32 us; the launch traced here: 31.9 us
  Pallas kernels  31.8 us (99%)
    pallas_call x1, Pallas kernels, per_device(): pl.pallas_call(functools.partial(exchange_kernel, chunks=chunks, gchunks=...  28.9 us
    pallas_call x1, Pallas kernels, per_device(): pl.pallas_call(place_kernel, out_shape=jax.ShapeDtypeStruct(object_delta....  2.99 us

profile of v2, /device:TPU:24, one launch (start us, length us, event | category | flops | bytes accessed | tf_op | source)
XLA Modules:
  0.0 31.9 jit_solution(3569276625949232943)
XLA Ops:
  0.0 28.9 %exchange.1 = (f32[2,1,2,256,256]{4,3,2,1,0:T(8,128)S(1)}, bf16[2,1,2,256,256]{4,3,2,1,0:T(8,128)(2,1)S(1)}, s32[2,2]{1,0:T(2,128)}) custom-call(f32[1,2,2048,256]{3,2,1,0:T(8,128)} %obj_hbm.1, bf16[2,256,256]{2,1,0:T(8,128)(2,1)} %probe_hbm.1, f32[2,256,256]{2,1,0:T(8,128)} %inten_hbm.1, s32[2,2]{1,0:T(2,128)} %pos.3, ...), custom_call_target="tpu_custom_call" | custom-call | tf_op jit(solution)/shard_map/exchange/pallas_call | solution.py:374
  28.9 3.0 %place.1 = f32[1,2,2048,256]{3,2,1,0:T(8,128)} custom-call(f32[2,1,2,256,256]{4,3,2,1,0:T(8,128)S(1)} %get-tuple-element.8.own, bf16[2,1,2,256,256]{4,3,2,1,0:T(8,128)(2,1)S(1)} %get-tuple-element.9.strip, s32[2,2]{1,0:T(2,128)} %pos.3, s32[2,2]{1,0:T(2,128)} %get-tuple-element.10.left), custom_call_target="tpu_custom_call" | custom-call | tf_op jit(solution)/shard_map/place/pallas_call | solution.py:410
